TPU v7x, 32 devices: a whole 2x2x4 slice. The times are simulated.
32 devices in a mesh: fsdp: 4 (over z), col: 8 (over y, x, core).
Axes of the slice: x: 2, y: 2, z: 4, core: 2. Of those that a mesh axis runs over, the one named last changes fastest.
Arguments:
- grad: float32 [8192, 28672], P(('fsdp', 'col')), may hold values from -40 to 40
- basis_old: float32 [8192, 512], P(('fsdp', 'col')), may hold values from -0.0625 to 0.0625
- moment: float32 [512, 28672], P('fsdp', 'col'), may hold values from -6 to 6
Outputs:
- lowrank_grad: float32 [512, 28672], P('fsdp', 'col')
- new_moment: float32 [512, 28672], P('fsdp', 'col')
All inputs are finite; a program needn't handle non-finite values.
Results may differ from a plain program's by a relative error of at most 0.017.
Values may be sent and summed in bfloat16 or wider, within the bound.
No kernel may reach another device: no remote copies, remote signals or barrier semaphores. Data moves between devices by JAX's collectives and lax.ppermute only.
A program may use at most 128 MiB of HBM per device.

v0:
```python
import jax
import jax.numpy as jnp
from jax import lax
from jax.sharding import PartitionSpec as P

R = 512
ITERS = 2
NS_STEPS = 5
schulz_a = 3.4445
schulz_b = -4.775
schulz_c = 2.0315


def orthogonal_sharded(image):
    highest = lax.Precision.HIGHEST
    scale = lax.psum(jnp.sum(image * image), ("fsdp", "col"))
    ortho = image / jnp.sqrt(scale)
    for schulz_step in range(NS_STEPS):
        gram = lax.psum(jnp.dot(ortho.T, ortho, precision=highest), ("fsdp", "col"))
        poly = schulz_b * gram + schulz_c * jnp.dot(gram, gram, precision=highest)
        ortho = schulz_a * ortho + jnp.dot(ortho, poly, precision=highest)
    return ortho


def local(grad, basis_old, moment):
    highest = lax.Precision.HIGHEST
    grad_tile = lax.all_to_all(
        grad.astype(jnp.bfloat16), "col", split_axis=1, concat_axis=0, tiled=True
    )
    basis = basis_old
    for iteration in range(ITERS):
        basis_half = basis.astype(jnp.bfloat16)
        partial_coeff = lax.dot_general(
            grad_tile,
            lax.all_gather(basis_half, "col", axis=0, tiled=True),
            (((0,), (0,)), ((), ())),
            preferred_element_type=jnp.float32,
        )
        coeff = lax.psum(partial_coeff.astype(jnp.bfloat16), "fsdp")
        image = lax.psum_scatter(
            jnp.dot(grad_tile, coeff, preferred_element_type=jnp.float32).astype(jnp.bfloat16),
            "col",
            scatter_dimension=0,
            tiled=True,
        ).astype(jnp.float32)
        basis = orthogonal_sharded(image)
    gathered = lax.all_gather(basis.astype(jnp.bfloat16), "col", axis=0, tiled=True)
    share = R // lax.axis_size("fsdp")
    lowrank_grad = lax.psum_scatter(
        lax.dot_general(
            gathered, grad_tile, (((0,), (0,)), ((), ())), preferred_element_type=jnp.float32
        ).astype(jnp.bfloat16),
        "fsdp",
        scatter_dimension=0,
        tiled=True,
    ).astype(jnp.float32)
    margin = lax.psum(jnp.dot(basis.T, basis_old, precision=highest), ("fsdp", "col"))
    own_block = lax.axis_index("fsdp")
    margin_rows = lax.dynamic_slice_in_dim(margin, own_block * share, share, 0)
    new_moment = jnp.zeros((share, moment.shape[1]), jnp.float32) + jnp.dot(
        margin_rows,
        lax.all_gather(moment.astype(jnp.bfloat16), "fsdp", axis=0, tiled=True).astype(jnp.float32),
        precision=highest,
    )
    return (lowrank_grad, new_moment)


def solution(mesh):
    placed = (P(("fsdp", "col"), None), P(("fsdp", "col"), None), P("fsdp", "col"))
    return jax.shard_map(
        local,
        mesh=mesh,
        in_specs=placed,
        out_specs=(P("fsdp", "col"), P("fsdp", "col")),
        check_vma=False,
    )
```

profile of v0, /device:TPU:0, one launch (start us, length us, event | category | flops | bytes accessed | tf_op | source)
XLA Modules:
  0.0 2444.1 jit_solution(9534226656882063459)
XLA Ops:
  7.2 23.0 copy.23
  30.2 5.7 all-to-all-start
  36.7 169.7 %all-to-all-done = bf16[256,8,3584]{0,2,1:T(8,128)(2,1)} async-done(((bf16[256,8,3584]{0,2,1:T(8,128)(2,1)}), bf16[256,8,3584]{0,2,1:T(8,128)(2,1)}, u32[]{:S(2)}, u32[]{:S(2)}) %all-to-all-start) | async-done | bytes 14680096 | tf_op jit(solution)/shard_map/all_to_all | solution.py:27
  206.5 18.8 copy.24
  225.2 13.0 convolution_convert_fusion.2
  238.3 138.3 %all-reduce.14.cloned.1.call-done = bf16[3584,512]{1,0:T(8,128)(2,1)} async-done(((bf16[3584,512]{1,0:T(8,128)(2,1)}), bf16[3584,512]{1,0:T(8,128)(2,1)}) %all-reduce.14.cloned.1.call-update) | async-done | bytes 3670032 | tf_op jit(solution)/shard_map/psum | solution.py:39
  376.5 13.2 fusion.1
  389.8 40.2 %reduce-scatter.4.cloned.1.call-done = bf16[256,512]{0,1:T(8,128)(2,1)} async-done(((bf16[2048,512]{0,1:T(8,128)(2,1)}), bf16[256,512]{0,1:T(8,128)(2,1)}) %reduce-scatter.4.cloned.1.call-update) | async-done | bytes 262160 | tf_op jit(solution)/shard_map/reduce_scatter | solution.py:40
  431.8 39.5 %psum.106 = f32[]{:T(128)} all-reduce(f32[]{:T(128)} %fusion.14), channel_id=1, replica_groups=mesh['fsdp'=4,'col'=8] {'fsdp','col'}, use_global_device_ids=true, to_apply=%region_3.0 | all-reduce | flops 1 | bytes 8 | tf_op jit(solution)/shard_map/psum | solution.py:16
  472.0 3.1 fusion.16
  475.7 131.2 %all-reduce.16.cloned.1.call-done = f32[512,512]{1,0:T(8,128)} async-done(((f32[512,512]{1,0:T(8,128)}), f32[512,512]{1,0:T(8,128)}) %all-reduce.16.cloned.1.call-update) | async-done | bytes 1048592 | tf_op jit(solution)/shard_map/psum | solution.py:19
  606.9 3.8 fusion.12
  612.6 2.0 fusion.26
  614.7 129.7 %all-reduce.18.cloned.1.call-done = f32[512,512]{1,0:T(8,128)} async-done(((f32[512,512]{1,0:T(8,128)}), f32[512,512]{1,0:T(8,128)}) %all-reduce.18.cloned.1.call-update) | async-done | bytes 1048592 | tf_op jit(solution)/shard_map/psum | solution.py:19
  744.4 3.8 fusion.11
  750.1 2.0 fusion.27
  752.3 129.6 %all-reduce.20.cloned.1.call-done = f32[512,512]{1,0:T(8,128)} async-done(((f32[512,512]{1,0:T(8,128)}), f32[512,512]{1,0:T(8,128)}) %all-reduce.20.cloned.1.call-update) | async-done | bytes 1048592 | tf_op jit(solution)/shard_map/psum | solution.py:19
  881.9 3.8 fusion.10
  889.7 129.7 %all-reduce.22.cloned.1.call-done = f32[512,512]{1,0:T(8,128)} async-done(((f32[512,512]{1,0:T(8,128)}), f32[512,512]{1,0:T(8,128)}) %all-reduce.22.cloned.1.call-update) | async-done | bytes 1048592 | tf_op jit(solution)/shard_map/psum | solution.py:19
  1019.4 3.8 fusion.9
  1027.4 129.5 %all-reduce.24.cloned.1.call-done = f32[512,512]{1,0:T(8,128)} async-done(((f32[512,512]{1,0:T(8,128)}), f32[512,512]{1,0:T(8,128)}) %all-reduce.24.cloned.1.call-update) | async-done | bytes 1048592 | tf_op jit(solution)/shard_map/psum | solution.py:19
  1156.9 3.8 fusion.8
  1160.8 2.5 fusion.13
  1163.4 27.2 %all-gather.7.cloned.1.call-done = bf16[2048,512]{0,1:T(8,128)(2,1)} async-done(((bf16[256,512]{0,1:T(8,128)(2,1)}), bf16[2048,512]{0,1:T(8,128)(2,1)}) %all-gather.7.cloned.1.call-update) | async-done | bytes 2097168 | tf_op jit(solution)/shard_map/all_gather | solution.py:35
  1190.5 12.9 fusion
  1203.5 138.1 %all-reduce.26.cloned.1.call-done = bf16[3584,512]{0,1:T(8,128)(2,1)} async-done(((bf16[3584,512]{0,1:T(8,128)(2,1)}), bf16[3584,512]{0,1:T(8,128)(2,1)}) %all-reduce.26.cloned.1.call-update) | async-done | bytes 3670032 | tf_op jit(solution)/shard_map/psum | solution.py:39
  1341.6 13.1 fusion.2
  1354.8 40.2 %reduce-scatter.6.cloned.1.call-done = bf16[256,512]{0,1:T(8,128)(2,1)} async-done(((bf16[2048,512]{0,1:T(8,128)(2,1)}), bf16[256,512]{0,1:T(8,128)(2,1)}) %reduce-scatter.6.cloned.1.call-update) | async-done | bytes 262160 | tf_op jit(solution)/shard_map/reduce_scatter | solution.py:40
  1396.8 39.5 %psum.113 = f32[]{:T(128)} all-reduce(f32[]{:T(128)} %fusion.15), channel_id=1, replica_groups=mesh['fsdp'=4,'col'=8] {'fsdp','col'}, use_global_device_ids=true, to_apply=%region_12.0 | all-reduce | flops 1 | bytes 8 | tf_op jit(solution)/shard_map/psum | solution.py:16
  1437.0 3.1 fusion.17
  1440.6 131.3 %all-reduce.28.cloned.1.call-done = f32[512,512]{1,0:T(8,128)} async-done(((f32[512,512]{1,0:T(8,128)}), f32[512,512]{1,0:T(8,128)}) %all-reduce.28.cloned.1.call-update) | async-done | bytes 1048592 | tf_op jit(solution)/shard_map/psum | solution.py:19
  1572.0 3.8 fusion.7
  1579.7 129.7 %all-reduce.30.cloned.1.call-done = f32[512,512]{1,0:T(8,128)} async-done(((f32[512,512]{1,0:T(8,128)}), f32[512,512]{1,0:T(8,128)}) %all-reduce.30.cloned.1.call-update) | async-done | bytes 1048592 | tf_op jit(solution)/shard_map/psum | solution.py:19
  1709.5 3.8 fusion.6
  1717.4 129.6 %all-reduce.32.cloned.1.call-done = f32[512,512]{1,0:T(8,128)} async-done(((f32[512,512]{1,0:T(8,128)}), f32[512,512]{1,0:T(8,128)}) %all-reduce.32.cloned.1.call-update) | async-done | bytes 1048592 | tf_op jit(solution)/shard_map/psum | solution.py:19
  1847.0 3.8 fusion.5
  1854.7 129.7 %all-reduce.34.cloned.1.call-done = f32[512,512]{1,0:T(8,128)} async-done(((f32[512,512]{1,0:T(8,128)}), f32[512,512]{1,0:T(8,128)}) %all-reduce.34.cloned.1.call-update) | async-done | bytes 1048592 | tf_op jit(solution)/shard_map/psum | solution.py:19
  1984.5 3.8 fusion.4
  1992.4 129.5 %all-reduce.36.cloned.1.call-done = f32[512,512]{1,0:T(8,128)} async-done(((f32[512,512]{1,0:T(8,128)}), f32[512,512]{1,0:T(8,128)}) %all-reduce.36.cloned.1.call-update) | async-done | bytes 1048592 | tf_op jit(solution)/shard_map/psum | solution.py:19
  2122.0 3.8 fusion.3
  2125.8 2.5 fusion.25
  2131.6 24.0 all-gather.9.cloned.1.call-done
  2155.5 12.9 convolution_convert_fusion
  2168.4 61.2 %all-gather.11.cloned.1.call-done = bf16[512,3584]{1,0:T(8,128)(2,1)} async-done(((bf16[128,3584]{1,0:T(8,128)(2,1)}), bf16[512,3584]{1,0:T(8,128)(2,1)}) %all-gather.11.cloned.1.call-update) | async-done | bytes 3670032 | tf_op jit(solution)/shard_map/all_gather | solution.py:62
  2229.7 135.1 %all-reduce.38.cloned.1.call-done = f32[512,512]{1,0:T(8,128)} async-done(((f32[512,512]{1,0:T(8,128)}), f32[512,512]{1,0:T(8,128)}) %all-reduce.38.cloned.1.call-update) | async-done | bytes 1048592 | tf_op jit(solution)/shard_map/psum | solution.py:57
  2364.7 5.0 fusion.18
  2369.7 64.7 %reduce-scatter.8.cloned.1.call-done = bf16[128,3584]{1,0:T(8,128)(2,1)} async-done(((bf16[512,3584]{1,0:T(8,128)(2,1)}), bf16[128,3584]{1,0:T(8,128)(2,1)}) %reduce-scatter.8.cloned.1.call-update) | async-done | bytes 917520 | tf_op jit(solution)/shard_map/reduce_scatter | solution.py:49
  2434.4 2.6 convert_element_type.63
  (68 shorter events, 36.7 us)
Async XLA Ops:
  30.2 5.7 copy-start
  30.2 176.3 %all-to-all-start = ((bf16[256,8,3584]{0,2,1:T(8,128)(2,1)}), bf16[256,8,3584]{0,2,1:T(8,128)(2,1)}, u32[]{:S(2)}, u32[]{:S(2)}) async-start(bf16[256,8,3584]{0,2,1:T(8,128)(2,1)} %bitcast.76), calls=%async_computation | async-start | bytes 29360128 | tf_op jit(solution)/shard_map/all_to_all | solution.py:27
  35.9 189.4 %all-gather.5.cloned.1.call-start = ((), (), s32[]{:S(2)}) async-start(), calls=%async_computation.4 | async-start | bytes 2359296 | tf_op jit(solution)/shard_map/all_gather | solution.py:35
  36.7 339.9 %all-reduce.14.cloned.1.call-start = ((), (), s32[]{:S(2)}) async-start(), calls=%async_computation.5 | async-start | bytes 7340032 | tf_op jit(solution)/shard_map/psum | solution.py:39
  238.2 191.8 %reduce-scatter.4.cloned.1.call-start = ((), (), s32[]{:S(2)}) async-start(), calls=%async_computation.6 | async-start | bytes 2359296 | tf_op jit(solution)/shard_map/reduce_scatter | solution.py:40
  389.8 217.1 %all-reduce.16.cloned.1.call-start = ((), (), s32[]{:S(2)}) async-start(), calls=%async_computation.7 | async-start | bytes 2097152 | tf_op jit(solution)/shard_map/psum | solution.py:19
  430.1 180.7 %copy-start.2 = (bf16[256,512]{0,1:T(8,128)(2,1)S(1)}, bf16[256,512]{0,1:T(8,128)(2,1)}, u32[]{:S(2)}) copy-start(bf16[256,512]{0,1:T(8,128)(2,1)} %reduce-scatter.4.cloned.1.call-done) | copy-start | bytes 786436
  475.2 269.3 %all-reduce.18.cloned.1.call-start = ((), (), s32[]{:S(2)}) async-start(), calls=%async_computation.8 | async-start | bytes 2097152 | tf_op jit(solution)/shard_map/psum | solution.py:19
  614.6 267.3 %all-reduce.20.cloned.1.call-start = ((), (), s32[]{:S(2)}) async-start(), calls=%async_computation.9 | async-start | bytes 2097152 | tf_op jit(solution)/shard_map/psum | solution.py:19
  752.1 267.3 %all-reduce.22.cloned.1.call-start = ((), (), s32[]{:S(2)}) async-start(), calls=%async_computation.10 | async-start | bytes 2097152 | tf_op jit(solution)/shard_map/psum | solution.py:19
  889.6 267.3 %all-reduce.24.cloned.1.call-start = ((), (), s32[]{:S(2)}) async-start(), calls=%async_computation.11 | async-start | bytes 2097152 | tf_op jit(solution)/shard_map/psum | solution.py:19
  1027.1 163.4 %all-gather.7.cloned.1.call-start = ((), (), s32[]{:S(2)}) async-start(), calls=%async_computation.12 | async-start | bytes 2359296 | tf_op jit(solution)/shard_map/all_gather | solution.py:35
  1163.3 178.3 %all-reduce.26.cloned.1.call-start = ((), (), s32[]{:S(2)}) async-start(), calls=%async_computation.13 | async-start | bytes 7340032 | tf_op jit(solution)/shard_map/psum | solution.py:39
  1203.4 191.6 %reduce-scatter.6.cloned.1.call-start = ((), (), s32[]{:S(2)}) async-start(), calls=%async_computation.14 | async-start | bytes 2359296 | tf_op jit(solution)/shard_map/reduce_scatter | solution.py:40
  1354.8 217.2 %all-reduce.28.cloned.1.call-start = ((), (), s32[]{:S(2)}) async-start(), calls=%async_computation.15 | async-start | bytes 2097152 | tf_op jit(solution)/shard_map/psum | solution.py:19
  1395.1 180.7 %copy-start.3 = (bf16[256,512]{0,1:T(8,128)(2,1)S(1)}, bf16[256,512]{0,1:T(8,128)(2,1)}, u32[]{:S(2)}) copy-start(bf16[256,512]{0,1:T(8,128)(2,1)} %reduce-scatter.6.cloned.1.call-done) | copy-start | bytes 786436
  1440.2 269.3 %all-reduce.30.cloned.1.call-start = ((), (), s32[]{:S(2)}) async-start(), calls=%async_computation.16 | async-start | bytes 2097152 | tf_op jit(solution)/shard_map/psum | solution.py:19
  1579.7 267.3 %all-reduce.32.cloned.1.call-start = ((), (), s32[]{:S(2)}) async-start(), calls=%async_computation.17 | async-start | bytes 2097152 | tf_op jit(solution)/shard_map/psum | solution.py:19
  1717.2 267.3 %all-reduce.34.cloned.1.call-start = ((), (), s32[]{:S(2)}) async-start(), calls=%async_computation.18 | async-start | bytes 2097152 | tf_op jit(solution)/shard_map/psum | solution.py:19
  1854.7 267.3 %all-reduce.36.cloned.1.call-start = ((), (), s32[]{:S(2)}) async-start(), calls=%async_computation.19 | async-start | bytes 2097152 | tf_op jit(solution)/shard_map/psum | solution.py:19
  1992.2 136.2 %copy-start.1 = (f32[128,3584]{1,0:T(8,128)S(1)}, f32[128,3584]{1,0:T(8,128)}, u32[]{:S(2)}) copy-start(f32[128,3584]{1,0:T(8,128)} %param.5) | copy-start | bytes 5505028
  1992.2 163.4 %all-gather.9.cloned.1.call-start = ((), (), s32[]{:S(2)}) async-start(), calls=%async_computation.20 | async-start | bytes 2359296 | tf_op jit(solution)/shard_map/all_gather | solution.py:47
  2128.3 101.3 %all-gather.11.cloned.1.call-start = ((), (), s32[]{:S(2)}) async-start(), calls=%async_computation.23 | async-start | bytes 4587520 | tf_op jit(solution)/shard_map/all_gather | solution.py:62
  2129.4 235.3 %all-reduce.38.cloned.1.call-start = ((), (), s32[]{:S(2)}) async-start(), calls=%async_computation.22 | async-start | bytes 2097152 | tf_op jit(solution)/shard_map/psum | solution.py:57
  2131.5 302.9 %reduce-scatter.8.cloned.1.call-start = ((), (), s32[]{:S(2)}) async-start(), calls=%async_computation.21 | async-start | bytes 4587520 | tf_op jit(solution)/shard_map/reduce_scatter | solution.py:49
Sparse Core Ops, SparseCore 0:
  39.1 95.7 all-gather.4
  238.4 138.1 all-reduce.13
  389.9 40.1 reduce-scatter.3
  475.3 131.5 all-reduce.15
  614.8 129.6 all-reduce.17
  752.2 129.6 all-reduce.19
  889.8 129.6 all-reduce.21
  1027.3 129.6 all-reduce.23
  1163.5 27.0 all-gather.6
  1203.6 138.0 all-reduce.25
  1354.9 40.1 reduce-scatter.5
  1440.3 131.6 all-reduce.27
  1579.8 129.6 all-reduce.29
  1717.3 129.6 all-reduce.31
  1854.8 129.6 all-reduce.33
  1992.3 129.6 all-reduce.35
  2128.5 27.0 all-gather.8
  2157.5 72.0 all-gather.10
  2235.4 129.2 all-reduce.37
  2366.9 67.4 reduce-scatter.7
where the time goes:
time: 2450 us; the launch traced here: 2440 us
  waiting for transfers between devices  2140 us (87%)
  matrix products  152 us (6%)
  blocking collectives  79 us (3%)
  local copies, waits for them, and re-layouts  41.8 us (2%)
    psum x10, waiting for transfers between devices, orthogonal_sharded(): gram = lax.psum(jnp.dot(ortho.T, ortho, precision=highest), ('fsdp', 'col'))  1300 us
    psum x2, waiting for transfers between devices, local(): coeff = lax.psum(partial_coeff.astype(jnp.bfloat16), 'fsdp')  276 us
    all_to_all x1, waiting for transfers between devices, local(): lax.all_to_all(grad.astype(jnp.bfloat16), 'col', split_axis=1, concat_axi...  170 us
    psum x1, waiting for transfers between devices, local(): lax.psum(jnp.dot(basis.T, basis_old, precision=highest), ('fsdp', 'col'))  135 us
    reduce_scatter x2, waiting for transfers between devices, local(): lax.psum_scatter(jnp.dot(grad_tile, coeff, preferred_element_type=jnp.flo...  80.5 us
    psum x2, blocking collectives, orthogonal_sharded(): scale = lax.psum(jnp.sum(image * image), ('fsdp', 'col'))  79 us
    reduce_scatter x1, waiting for transfers between devices, local(): lax.psum_scatter(lax.dot_general(gathered, grad_tile, (((0,), (0,)), ((),...  64.7 us
    all_gather x1, waiting for transfers between devices, local(): lax.all_gather(moment.astype(jnp.bfloat16), 'fsdp', axis=0, tiled=True)  61.2 us
  transfers between devices with their start and end apart: 21, of which 20 were waited for; matrix products, arithmetic and copies ran while one was open for 2% of the time, Pallas kernels for 0%

commit v1 on v0

--- a/solution.py
+++ b/solution.py
@@ -36,7 +36,9 @@
             (((0,), (0,)), ((), ())),
             preferred_element_type=jnp.float32,
         )
-        coeff = lax.psum(partial_coeff.astype(jnp.bfloat16), "fsdp")
+        own = partial_coeff.astype(jnp.bfloat16)
+        terms = lax.all_gather(own, "fsdp")
+        coeff = jnp.sum(terms, axis=0)
         image = lax.psum_scatter(
             jnp.dot(grad_tile, coeff, preferred_element_type=jnp.float32).astype(jnp.bfloat16),
             "col",

time: 2450 us -> 2740 us (1.12)
  waiting for transfers between devices: 2140 us -> 2370 us
  other arithmetic: 7.86 us -> 43.3 us
  local copies, waits for them, and re-layouts: 41.8 us -> 69.5 us
    all_gather x0 -> x2, waiting for transfers between devices: none -> 505 us  [local(): terms = lax.all_gather(own, 'fsdp')]
    psum x2 -> x0, waiting for transfers between devices: 276 us -> none  [local(): coeff = lax.psum(partial_coeff.astype(jnp.bfloat16), 'fsdp')]
    reduce_sum x0 -> x2, other arithmetic: none -> 35.5 us  [local(): coeff = jnp.sum(terms, axis=0)]
    all_gather x0 -> x1, local copies, waits for them, and re-layouts: none -> 27.6 us  [local(): terms = lax.all_gather(own, 'fsdp')]
  transfers between devices with their start and end apart: 21 -> 21, of which waited for: 20 -> 20; matrix products, arithmetic and copies ran while one was open for 2% -> 1% of each run, Pallas kernels for 0% -> 0%
where the time goes in v1:
time: 2740 us; the launch traced here: 2730 us
  waiting for transfers between devices  2370 us (86%)
  matrix products  152 us (6%)
  blocking collectives  79.4 us (3%)
  local copies, waits for them, and re-layouts  69.5 us (3%)
  other arithmetic  43.3 us (2%)
    psum x10, waiting for transfers between devices, orthogonal_sharded(): gram = lax.psum(jnp.dot(ortho.T, ortho, precision=highest), ('fsdp', 'col'))  1300 us
    all_gather x2, waiting for transfers between devices, local(): terms = lax.all_gather(own, 'fsdp')  505 us
    all_to_all x1, waiting for transfers between devices, local(): lax.all_to_all(grad.astype(jnp.bfloat16), 'col', split_axis=1, concat_axi...  170 us
    psum x1, waiting for transfers between devices, local(): lax.psum(jnp.dot(basis.T, basis_old, precision=highest), ('fsdp', 'col'))  135 us
    psum x2, blocking collectives, orthogonal_sharded(): scale = lax.psum(jnp.sum(image * image), ('fsdp', 'col'))  79.4 us
    reduce_scatter x2, waiting for transfers between devices, local(): lax.psum_scatter(jnp.dot(grad_tile, coeff, preferred_element_type=jnp.flo...  78.8 us
    reduce_scatter x1, waiting for transfers between devices, local(): lax.psum_scatter(lax.dot_general(gathered, grad_tile, (((0,), (0,)), ((),...  64.7 us
    all_gather x1, waiting for transfers between devices, local(): lax.all_gather(moment.astype(jnp.bfloat16), 'fsdp', axis=0, tiled=True)  61.2 us
  transfers between devices with their start and end apart: 21, of which 20 were waited for; matrix products, arithmetic and copies ran while one was open for 1% of the time, Pallas kernels for 0%

profile of v1, /device:TPU:0, one launch (start us, length us, event | category | flops | bytes accessed | tf_op | source)
XLA Modules:
  0.0 2734.6 jit_solution(17935298463080463558)
XLA Ops:
  7.2 23.0 copy.35
  30.2 5.7 all-to-all-start
  36.7 169.7 %all-to-all-done = bf16[256,8,3584]{0,2,1:T(8,128)(2,1)} async-done(((bf16[256,8,3584]{0,2,1:T(8,128)(2,1)}), bf16[256,8,3584]{0,2,1:T(8,128)(2,1)}, u32[]{:S(2)}, u32[]{:S(2)}) %all-to-all-start) | async-done | bytes 14680096 | tf_op jit(solution)/shard_map/all_to_all | solution.py:27
  206.5 18.8 copy.36
  225.2 12.9 convolution_convert_fusion.2
  238.3 252.7 %all-gather.17.cloned.1.call-done = bf16[14336,512]{1,0:T(8,128)(2,1)} async-done(((bf16[3584,512]{1,0:T(8,128)(2,1)}), bf16[14336,512]{1,0:T(8,128)(2,1)}) %all-gather.17.cloned.1.call-update) | async-done | bytes 14680080 | tf_op jit(solution)/shard_map/all_gather | solution.py:40
  491.0 10.7 reduce_sum.42
  501.6 13.2 fusion.1
  514.9 39.4 %reduce-scatter.4.cloned.1.call-done = bf16[256,512]{0,1:T(8,128)(2,1)} async-done(((bf16[2048,512]{0,1:T(8,128)(2,1)}), bf16[256,512]{0,1:T(8,128)(2,1)}) %reduce-scatter.4.cloned.1.call-update) | async-done | bytes 262160 | tf_op jit(solution)/shard_map/reduce_scatter | solution.py:42
  556.1 39.9 %psum.91 = f32[]{:T(128)} all-reduce(f32[]{:T(128)} %fusion.14), channel_id=1, replica_groups=mesh['fsdp'=4,'col'=8] {'fsdp','col'}, use_global_device_ids=true, to_apply=%region_3.0 | all-reduce | flops 1 | bytes 8 | tf_op jit(solution)/shard_map/psum | solution.py:16
  596.7 3.1 fusion.16
  599.8 131.7 %all-reduce.12.cloned.1.call-done = f32[512,512]{1,0:T(8,128)} async-done(((f32[512,512]{1,0:T(8,128)}), f32[512,512]{1,0:T(8,128)}) %all-reduce.12.cloned.1.call-update) | async-done | bytes 1048592 | tf_op jit(solution)/shard_map/psum | solution.py:19
  731.5 3.8 fusion.12
  739.3 129.7 %all-reduce.14.cloned.1.call-done = f32[512,512]{1,0:T(8,128)} async-done(((f32[512,512]{1,0:T(8,128)}), f32[512,512]{1,0:T(8,128)}) %all-reduce.14.cloned.1.call-update) | async-done | bytes 1048592 | tf_op jit(solution)/shard_map/psum | solution.py:19
  869.0 3.8 fusion.11
  876.9 129.6 %all-reduce.16.cloned.1.call-done = f32[512,512]{1,0:T(8,128)} async-done(((f32[512,512]{1,0:T(8,128)}), f32[512,512]{1,0:T(8,128)}) %all-reduce.16.cloned.1.call-update) | async-done | bytes 1048592 | tf_op jit(solution)/shard_map/psum | solution.py:19
  1006.5 3.8 fusion.10
  1014.3 129.7 %all-reduce.18.cloned.1.call-done = f32[512,512]{1,0:T(8,128)} async-done(((f32[512,512]{1,0:T(8,128)}), f32[512,512]{1,0:T(8,128)}) %all-reduce.18.cloned.1.call-update) | async-done | bytes 1048592 | tf_op jit(solution)/shard_map/psum | solution.py:19
  1144.0 3.8 fusion.9
  1152.0 129.5 %all-reduce.20.cloned.1.call-done = f32[512,512]{1,0:T(8,128)} async-done(((f32[512,512]{1,0:T(8,128)}), f32[512,512]{1,0:T(8,128)}) %all-reduce.20.cloned.1.call-update) | async-done | bytes 1048592 | tf_op jit(solution)/shard_map/psum | solution.py:19
  1281.5 3.8 fusion.8
  1285.3 2.5 fusion.13
  1287.9 27.2 all-gather.11.cloned.1.call-done
  1315.1 12.9 fusion
  1328.3 252.3 %all-gather.19.cloned.1.call-done = bf16[14336,512]{0,1:T(8,128)(2,1)} async-done(((bf16[3584,512]{0,1:T(8,128)(2,1)}), bf16[14336,512]{0,1:T(8,128)(2,1)}) %all-gather.19.cloned.1.call-update) | async-done | bytes 14680080 | tf_op jit(solution)/shard_map/all_gather | solution.py:40
  1580.6 27.6 %reshape.8 = bf16[4,3584,512]{1,0,2:T(4,128)(2,1)} reshape(bf16[14336,512]{0,1:T(8,128)(2,1)} %all-gather.19.cloned.1.call-done) | data formatting | bytes 29360128 | tf_op jit(solution)/shard_map/all_gather | solution.py:40
  1608.2 24.8 reduce_sum.44
  1633.1 13.2 fusion.2
  1646.3 39.4 %reduce-scatter.6.cloned.1.call-done = bf16[256,512]{0,1:T(8,128)(2,1)} async-done(((bf16[2048,512]{0,1:T(8,128)(2,1)}), bf16[256,512]{0,1:T(8,128)(2,1)}) %reduce-scatter.6.cloned.1.call-update) | async-done | bytes 262160 | tf_op jit(solution)/shard_map/reduce_scatter | solution.py:42
  1687.5 39.5 %psum.97 = f32[]{:T(128)} all-reduce(f32[]{:T(128)} %fusion.15), channel_id=1, replica_groups=mesh['fsdp'=4,'col'=8] {'fsdp','col'}, use_global_device_ids=true, to_apply=%region_12.0 | all-reduce | flops 1 | bytes 8 | tf_op jit(solution)/shard_map/psum | solution.py:16
  1727.6 3.1 fusion.17
  1731.3 131.3 %all-reduce.22.cloned.1.call-done = f32[512,512]{1,0:T(8,128)} async-done(((f32[512,512]{1,0:T(8,128)}), f32[512,512]{1,0:T(8,128)}) %all-reduce.22.cloned.1.call-update) | async-done | bytes 1048592 | tf_op jit(solution)/shard_map/psum | solution.py:19
  1862.6 3.8 fusion.7
  1870.4 129.7 %all-reduce.24.cloned.1.call-done = f32[512,512]{1,0:T(8,128)} async-done(((f32[512,512]{1,0:T(8,128)}), f32[512,512]{1,0:T(8,128)}) %all-reduce.24.cloned.1.call-update) | async-done | bytes 1048592 | tf_op jit(solution)/shard_map/psum | solution.py:19
  2000.1 3.8 fusion.6
  2008.0 129.6 %all-reduce.26.cloned.1.call-done = f32[512,512]{1,0:T(8,128)} async-done(((f32[512,512]{1,0:T(8,128)}), f32[512,512]{1,0:T(8,128)}) %all-reduce.26.cloned.1.call-update) | async-done | bytes 1048592 | tf_op jit(solution)/shard_map/psum | solution.py:19
  2137.6 3.8 fusion.5
  2145.3 129.7 %all-reduce.28.cloned.1.call-done = f32[512,512]{1,0:T(8,128)} async-done(((f32[512,512]{1,0:T(8,128)}), f32[512,512]{1,0:T(8,128)}) %all-reduce.28.cloned.1.call-update) | async-done | bytes 1048592 | tf_op jit(solution)/shard_map/psum | solution.py:19
  2275.1 3.8 fusion.4
  2283.1 129.5 %all-reduce.30.cloned.1.call-done = f32[512,512]{1,0:T(8,128)} async-done(((f32[512,512]{1,0:T(8,128)}), f32[512,512]{1,0:T(8,128)}) %all-reduce.30.cloned.1.call-update) | async-done | bytes 1048592 | tf_op jit(solution)/shard_map/psum | solution.py:19
  2412.6 3.8 fusion.3
  2422.2 24.0 all-gather.13.cloned.1.call-done
  2446.2 12.9 convolution_convert_fusion
  2459.1 61.2 %all-gather.15.cloned.1.call-done = bf16[512,3584]{1,0:T(8,128)(2,1)} async-done(((bf16[128,3584]{1,0:T(8,128)(2,1)}), bf16[512,3584]{1,0:T(8,128)(2,1)}) %all-gather.15.cloned.1.call-update) | async-done | bytes 3670032 | tf_op jit(solution)/shard_map/all_gather | solution.py:64
  2520.3 135.0 %all-reduce.32.cloned.1.call-done = f32[512,512]{1,0:T(8,128)} async-done(((f32[512,512]{1,0:T(8,128)}), f32[512,512]{1,0:T(8,128)}) %all-reduce.32.cloned.1.call-update) | async-done | bytes 1048592 | tf_op jit(solution)/shard_map/psum | solution.py:59
  2655.3 5.0 fusion.18
  2660.2 64.7 %reduce-scatter.8.cloned.1.call-done = bf16[128,3584]{1,0:T(8,128)(2,1)} async-done(((bf16[512,3584]{1,0:T(8,128)(2,1)}), bf16[128,3584]{1,0:T(8,128)(2,1)}) %reduce-scatter.8.cloned.1.call-update) | async-done | bytes 917520 | tf_op jit(solution)/shard_map/reduce_scatter | solution.py:51
  2724.9 2.6 convert_element_type.67
  (71 shorter events, 43.1 us)
Async XLA Ops:
  30.2 5.7 copy-start
  30.2 176.3 %all-to-all-start = ((bf16[256,8,3584]{0,2,1:T(8,128)(2,1)}), bf16[256,8,3584]{0,2,1:T(8,128)(2,1)}, u32[]{:S(2)}, u32[]{:S(2)}) async-start(bf16[256,8,3584]{0,2,1:T(8,128)(2,1)} %bitcast.79), calls=%async_computation | async-start | bytes 29360128 | tf_op jit(solution)/shard_map/all_to_all | solution.py:27
  35.9 189.4 %all-gather.9.cloned.1.call-start = ((), (), s32[]{:S(2)}) async-start(), calls=%async_computation.4 | async-start | bytes 2359296 | tf_op jit(solution)/shard_map/all_gather | solution.py:35
  36.7 454.3 %all-gather.17.cloned.1.call-start = ((), (), s32[]{:S(2)}) async-start(), calls=%async_computation.22 | async-start | bytes 18350080 | tf_op jit(solution)/shard_map/all_gather | solution.py:40
  238.2 316.1 %reduce-scatter.4.cloned.1.call-start = ((), (), s32[]{:S(2)}) async-start(), calls=%async_computation.5 | async-start | bytes 2359296 | tf_op jit(solution)/shard_map/reduce_scatter | solution.py:42
  514.8 216.7 %all-reduce.12.cloned.1.call-start = ((), (), s32[]{:S(2)}) async-start(), calls=%async_computation.6 | async-start | bytes 2097152 | tf_op jit(solution)/shard_map/psum | solution.py:19
  554.3 181.1 %copy-start.2 = (bf16[256,512]{0,1:T(8,128)(2,1)S(1)}, bf16[256,512]{0,1:T(8,128)(2,1)}, u32[]{:S(2)}) copy-start(bf16[256,512]{0,1:T(8,128)(2,1)} %reduce-scatter.4.cloned.1.call-done) | copy-start | bytes 786436
  599.8 269.2 %all-reduce.14.cloned.1.call-start = ((), (), s32[]{:S(2)}) async-start(), calls=%async_computation.7 | async-start | bytes 2097152 | tf_op jit(solution)/shard_map/psum | solution.py:19
  739.2 267.3 %all-reduce.16.cloned.1.call-start = ((), (), s32[]{:S(2)}) async-start(), calls=%async_computation.8 | async-start | bytes 2097152 | tf_op jit(solution)/shard_map/psum | solution.py:19
  876.7 267.3 %all-reduce.18.cloned.1.call-start = ((), (), s32[]{:S(2)}) async-start(), calls=%async_computation.9 | async-start | bytes 2097152 | tf_op jit(solution)/shard_map/psum | solution.py:19
  1014.2 267.3 %all-reduce.20.cloned.1.call-start = ((), (), s32[]{:S(2)}) async-start(), calls=%async_computation.10 | async-start | bytes 2097152 | tf_op jit(solution)/shard_map/psum | solution.py:19
  1151.7 163.4 %all-gather.11.cloned.1.call-start = ((), (), s32[]{:S(2)}) async-start(), calls=%async_computation.11 | async-start | bytes 2359296 | tf_op jit(solution)/shard_map/all_gather | solution.py:35
  1287.9 292.7 %all-gather.19.cloned.1.call-start = ((), (), s32[]{:S(2)}) async-start(), calls=%async_computation.23 | async-start | bytes 18350080 | tf_op jit(solution)/shard_map/all_gather | solution.py:40
  1328.0 357.7 %reduce-scatter.6.cloned.1.call-start = ((), (), s32[]{:S(2)}) async-start(), calls=%async_computation.12 | async-start | bytes 2359296 | tf_op jit(solution)/shard_map/reduce_scatter | solution.py:42
  1646.2 216.4 %all-reduce.22.cloned.1.call-start = ((), (), s32[]{:S(2)}) async-start(), calls=%async_computation.13 | async-start | bytes 2097152 | tf_op jit(solution)/shard_map/psum | solution.py:19
  1685.7 180.7 %copy-start.3 = (bf16[256,512]{0,1:T(8,128)(2,1)S(1)}, bf16[256,512]{0,1:T(8,128)(2,1)}, u32[]{:S(2)}) copy-start(bf16[256,512]{0,1:T(8,128)(2,1)} %reduce-scatter.6.cloned.1.call-done) | copy-start | bytes 786436
  1730.8 269.3 %all-reduce.24.cloned.1.call-start = ((), (), s32[]{:S(2)}) async-start(), calls=%async_computation.14 | async-start | bytes 2097152 | tf_op jit(solution)/shard_map/psum | solution.py:19
  1870.3 267.3 %all-reduce.26.cloned.1.call-start = ((), (), s32[]{:S(2)}) async-start(), calls=%async_computation.15 | async-start | bytes 2097152 | tf_op jit(solution)/shard_map/psum | solution.py:19
  2007.8 267.3 %all-reduce.28.cloned.1.call-start = ((), (), s32[]{:S(2)}) async-start(), calls=%async_computation.16 | async-start | bytes 2097152 | tf_op jit(solution)/shard_map/psum | solution.py:19
  2145.3 267.3 %all-reduce.30.cloned.1.call-start = ((), (), s32[]{:S(2)}) async-start(), calls=%async_computation.17 | async-start | bytes 2097152 | tf_op jit(solution)/shard_map/psum | solution.py:19
  2282.8 136.2 %copy-start.1 = (f32[128,3584]{1,0:T(8,128)S(1)}, f32[128,3584]{1,0:T(8,128)}, u32[]{:S(2)}) copy-start(f32[128,3584]{1,0:T(8,128)} %param.5) | copy-start | bytes 5505028
  2282.8 163.4 %all-gather.13.cloned.1.call-start = ((), (), s32[]{:S(2)}) async-start(), calls=%async_computation.18 | async-start | bytes 2359296 | tf_op jit(solution)/shard_map/all_gather | solution.py:49
  2419.0 101.3 %all-gather.15.cloned.1.call-start = ((), (), s32[]{:S(2)}) async-start(), calls=%async_computation.21 | async-start | bytes 4587520 | tf_op jit(solution)/shard_map/all_gather | solution.py:64
  2420.1 235.2 %all-reduce.32.cloned.1.call-start = ((), (), s32[]{:S(2)}) async-start(), calls=%async_computation.20 | async-start | bytes 2097152 | tf_op jit(solution)/shard_map/psum | solution.py:59
  2422.1 302.8 %reduce-scatter.8.cloned.1.call-start = ((), (), s32[]{:S(2)}) async-start(), calls=%async_computation.19 | async-start | bytes 4587520 | tf_op jit(solution)/shard_map/reduce_scatter | solution.py:51
Sparse Core Ops, SparseCore 0:
  39.1 95.7 all-gather.8
  238.3 252.6 all-gather.16
  514.9 39.2 reduce-scatter.3
  599.9 131.5 all-reduce.11
  739.3 129.6 all-reduce.13
  876.8 129.6 all-reduce.15
  1014.3 129.6 all-reduce.17
  1151.8 129.6 all-reduce.19
  1288.0 27.0 all-gather.10
  1328.1 252.4 all-gather.18
  1646.4 39.2 reduce-scatter.5
  1730.9 131.6 all-reduce.21
  1870.4 129.6 all-reduce.23
  2007.9 129.6 all-reduce.25
  2145.4 129.6 all-reduce.27
  2282.9 129.6 all-reduce.29
  2419.1 27.0 all-gather.12
  2448.2 72.0 all-gather.14
  2526.0 129.1 all-reduce.31
  2657.4 67.4 reduce-scatter.7
